TPU v7x, 128 devices: a whole 4x4x4 slice. The times are simulated.
128 devices in a mesh: dev: 16 (over z_hi, y, core), ha: 8 (over z_lo, x).
Axes of the slice: x: 4, y: 4, z: 4 (z_hi: 2, z_lo: 2; z = z_hi * 2 + z_lo), core: 2. Of those that a mesh axis runs over, the one named last changes fastest.
Arguments:
- volume: bfloat16 [4, 128, 128, 512], P(None, 'dev', 'ha'), may hold values from -6 to 6
- w_first: bfloat16 [3, 3, 3, 4, 32], replicated, may hold values from -0.625 to 0.625
- w_second: bfloat16 [3, 3, 3, 32, 64], replicated, may hold values from -0.21875 to 0.21875
- w_third: bfloat16 [3, 3, 3, 64, 128], P(None, None, None, None, 'ha'), may hold values from -0.15625 to 0.15625
- cotangent: bfloat16 [128, 16, 16, 64], P('ha', 'dev'), may hold values from -6 to 6
Outputs:
- out_third: bfloat16 [128, 16, 16, 64], P('ha', 'dev')
- grad_first: float32 [3, 3, 3, 4, 32], replicated
- grad_second: float32 [3, 3, 3, 32, 64], replicated
- grad_third: float32 [3, 3, 3, 64, 128], P(None, None, None, None, 'ha')
All inputs are finite; a program needn't handle non-finite values.
Results may differ from a plain program's by a relative error of at most 0.0063.
Values may be sent and summed in bfloat16 or wider, within the bound.
A program may use at most 192 MiB of HBM per device.

v0:
```python
import math
import jax
import jax.numpy as jnp
from jax import lax
from jax.sharding import PartitionSpec as P


def shifted(block, axis, distance):
    devices = range(lax.axis_size(axis))
    route = [(i - distance, i) for i in devices if i - distance in devices]
    return lax.ppermute(block, axis, route)


def leaky_relu(values):
    return 0.3 * values + 0.175 * jax.nn.softplus(4.0 * values)


def leaky_slope(values):
    return 0.3 + 0.7 * jax.nn.sigmoid(4.0 * values)


def convolve(inputs, kernel, pad_depth, pad_height):
    return lax.conv_general_dilated(
        inputs[None],
        kernel,
        (2, 2, 2),
        [pad_depth, pad_height, (1, 0)],
        dimension_numbers=("NCDHW", "DHWIO", "NCDHW"),
        preferred_element_type=jnp.float32,
    )[0]


def weight_grad(inputs, delta, pad_depth, pad_height):
    result = lax.conv_general_dilated(
        inputs[:, None],
        delta[:, None],
        (1, 1, 1),
        [pad_depth, pad_height, (1, 0)],
        rhs_dilation=(2, 2, 2),
        dimension_numbers=("NCDHW", "OIDHW", "NCDHW"),
        preferred_element_type=jnp.float32,
    )
    return jnp.transpose(result, (2, 3, 4, 0, 1))


def input_grad(delta, kernel):
    flipped = jnp.flip(kernel, (0, 1, 2))
    return lax.conv_general_dilated(
        delta[None],
        flipped,
        (1, 1, 1),
        [(2, 2)] * 3,
        lhs_dilation=(2, 2, 2),
        dimension_numbers=("NCDHW", "DHWOI", "NCDHW"),
        preferred_element_type=jnp.float32,
    )[0]


def extend_depth(values):
    lower = shifted(values[:, -1:], "dev", 1)
    return jnp.concatenate([lower, values], 1)


def extend(values):
    deeper = extend_depth(values)
    beside = shifted(deeper[:, :, -1:], "ha", 1)
    return jnp.concatenate([beside, deeper], 2)


def retract_depth(grads):
    lower = shifted(grads[:, 0:1], "dev", -1)
    inner = grads[:, 1:]
    return inner.at[:, -1:].add(lower)


def retract(grads):
    beside = shifted(grads[:, :, 0:1].astype(jnp.bfloat16), "ha", -1).astype(jnp.float32)
    inner = grads[:, :, 1:]
    inner = inner.at[:, :, -1:].add(beside)
    return retract_depth(inner)


def local(volume, w_first, w_second, w_third, cotangent):
    depth_total = volume.shape[1] * lax.axis_size("dev")
    height_total = volume.shape[2] * lax.axis_size("ha")
    width_total = volume.shape[3]
    scale_first = 1.0 / math.sqrt(depth_total // 2 * (height_total // 2) * (width_total // 2))
    scale_second = 1.0 / math.sqrt(depth_total // 4 * (height_total // 4) * (width_total // 4))
    scale_third = 1.0 / math.sqrt(depth_total // 8 * (height_total // 8) * (width_total // 8))
    whole_first = extend(volume)
    pre_first = convolve(whole_first, w_first, (0, 0), (0, 0))
    act_first = leaky_relu(pre_first).astype(jnp.bfloat16)
    whole_second = extend(act_first)
    pre_second = convolve(whole_second, w_second, (0, 0), (0, 0))
    act_second = leaky_relu(pre_second).astype(jnp.bfloat16)
    deeper = extend_depth(act_second)
    all_rows = lax.all_gather(deeper, "ha", axis=2, tiled=True)
    pre_third = convolve(all_rows, w_third, (0, 0), (1, 0))
    out_third = leaky_relu(pre_third).astype(jnp.bfloat16)
    delta_third = (cotangent.astype(jnp.float32) * leaky_slope(pre_third)).astype(jnp.bfloat16)
    grad_third = lax.psum(weight_grad(all_rows, delta_third, (0, 0), (1, 0)), "dev") * scale_third
    partial_back = input_grad(delta_third, w_third)[:, :, 1:, 1:]
    summed_back = lax.psum_scatter(partial_back, "ha", scatter_dimension=2, tiled=True)
    back_second = retract_depth(summed_back)
    delta_second = (back_second * leaky_slope(pre_second)).astype(jnp.bfloat16)
    local_second = weight_grad(whole_second, delta_second, (0, 0), (0, 0))
    back_first = retract(input_grad(delta_second, w_second)[..., 1:])
    delta_first = (back_first * leaky_slope(pre_first)).astype(jnp.bfloat16)
    local_first = weight_grad(whole_first, delta_first, (0, 0), (0, 0))
    grad_first, grad_second = lax.psum((local_first, local_second), ("dev", "ha"))
    return (out_third, grad_first * scale_first, grad_second * scale_second, grad_third)


def solution(mesh):
    placed = (
        P(None, "dev", "ha", None),
        P(),
        P(),
        P(None, None, None, None, "ha"),
        P("ha", "dev", None, None),
    )
    return jax.shard_map(
        local,
        mesh=mesh,
        in_specs=placed,
        out_specs=(P("ha", "dev", None, None), P(), P(), P(None, None, None, None, "ha")),
        check_vma=False,
    )
```

profile of v0, /device:TPU:1, one launch (start us, length us, event | category | flops | bytes accessed | tf_op | source)
XLA Modules:
  0.0 800.9 jit_solution(4794022419760191605)
XLA Ops:
  8.1 4.6 collective-permute-start
  15.2 3.1 collective-permute-start.1
  22.9 10.8 %copy.123 = bf16[4,9,17,1,8,66]{4,0,5,2,1,3:T(4,128)(2,1)} copy(bf16[4,9,17,1,8,66]{5,4,2,1,0,3:T(8,128)(2,1)S(1)} %reshape.287) | data formatting | bytes 1292544 | tf_op jit(solution)/shard_map/conv_general_dilated | solution.py:23
  35.0 32.7 %fusion.3 = f32[4,8,8,33,32]{4,2,3,1,0:T(8,128)} fusion(bf16[3,3,3,4,32]{4,3,2,1,0:T(4,128)(2,1)S(1)} %copy-done.15, bf16[4,9,17,1,7,2]{4,0,5,2,1,3:T(4,128)(2,1)S(1)} %slice.159, bf16[4,9,17,1,8,66]{4,0,5,2,1,3:T(4,128)(2,1)} %copy.123), kind=kOutput, calls=%fused_computation.4 | convolution fusion | flops 60390144 | bytes 1751664 | tf_op jit(solution)/shard_map/conv_general_dilated | solution.py:23
  67.7 18.2 %copy.124 = f32[4,8,8,33,32]{3,4,2,1,0:T(8,128)} copy(f32[4,8,8,33,32]{4,2,3,1,0:T(8,128)} %fusion.3) | data formatting | bytes 2162688 | tf_op jit(solution)/shard_map/conv_general_dilated | solution.py:23
  85.9 5.1 select_multiply_fusion
  91.0 5.9 copy.126
  96.9 3.5 reshape.226
  100.4 8.6 %copy.125 = f32[4,8,8,33,32]{3,2,4,1,0:T(8,128)} copy(f32[4,8,8,33,32]{3,4,2,1,0:T(8,128)} %get-tuple-element.53) | data formatting | bytes 2162688 | tf_op jit(solution)/shard_map/mul | solution.py:15
  109.0 3.5 reshape.224
  113.2 5.1 collective-permute-start.2
  118.3 1.9 collective-permute-done.2
  120.2 4.0 collective-permute-start.3
  128.1 4.0 reshape.229
  132.1 4.5 copy.128
  137.7 3.7 broadcast_multiply_fusion.2
  143.1 5.2 collective-permute-start.4
  148.3 1.9 collective-permute-done.4
  151.5 48.0 %all-gather.2.cloned.1.call-done = bf16[64,3,32,128]{3,0,1,2:T(8,128)(2,1)} async-done(((bf16[64,3,4,128]{3,0,1,2:T(8,128)(2,1)}), bf16[64,3,32,128]{3,0,1,2:T(8,128)(2,1)}) %all-gather.2.cloned.1.call-update) | async-done | bytes 1572880 | tf_op jit(solution)/shard_map/all_gather | solution.py:97
  199.5 5.8 copy.132
  205.9 2.3 copy.134
  208.4 2.2 broadcast_multiply_fusion
  212.9 4.3 broadcast_select_fusion
  217.1 5.8 copy.143
  223.0 9.0 %reshape.251 = f32[3,33,1,144,64]{4,3,1,0,2:T(8,128)} reshape(f32[3,33,8,18,64]{4,3,2,1,0:T(8,128)} %copy.143) | data formatting | bytes 7299072 | tf_op jit(solution)/shard_map/conv_general_dilated | solution.py:48
  231.9 3.4 slice_bitcast_fusion
  235.3 3.7 slice.172
  239.1 6.2 copy.144
  245.3 56.0 %copy.151 = bf16[4,1,9,17,512]{0,1,4,3,2:T(2,128)(2,1)} copy(bf16[4,1,9,17,512]{4,3,2,0,1:T(8,128)(2,1)S(1)} %copy-done.8) | data formatting | bytes 1253376 | tf_op jit(solution)/shard_map/broadcast_in_dim | solution.py:35
  301.3 8.8 %copy.153 = bf16[32,1,5,9,256]{0,1,4,3,2:T(2,128)(2,1)} copy(bf16[32,1,5,9,256]{4,0,3,2,1:T(8,128)(2,1)S(1)} %copy-done.9) | data formatting | bytes 1474560 | tf_op jit(solution)/shard_map/broadcast_in_dim | solution.py:35
  310.6 10.5 %copy.156 = bf16[64,1,3,32,128]{0,1,4,3,2:T(2,128)(2,1)} copy(bf16[64,1,3,32,128]{4,0,2,3,1:T(8,128)(2,1)S(1)} %bitcast.160) | data formatting | bytes 3145728 | tf_op jit(solution)/shard_map/broadcast_in_dim | solution.py:35
  322.3 8.7 %collective-permute-start.5 = (f32[64,1,4,128]{0,2,3,1:T(4,128)S(1)}, f32[64,1,4,128]{0,2,3,1:T(4,128)S(1)}, u32[]{:S(2)}, u32[]{:S(2)}) collective-permute-start(f32[64,1,4,128]{0,2,3,1:T(4,128)S(1)} %copy.168), channel_id=1, source_target_pairs={{8,0},{16,8},{24,16},{32,24},{40,32},{48,40},{56,48},{64,56},{72,6... | collective-permute-start | bytes 393224 | tf_op jit(solution)/shard_map/ppermute | solution.py:11
  331.0 15.7 %fusion.86 = f32[3,3,3,64,16]{3,4,2,1,0:T(8,128)} fusion(bf16[64,1,3,32,128]{0,1,4,3,2:T(2,128)(2,1)} %copy.156, bf16[16,1,1,16,64]{0,1,4,3,2:T(2,128)(2,1)S(1)} %copy.157), kind=kOutput, calls=%fused_computation.117 | convolution fusion | flops 55154688 | bytes 1716224 | tf_op jit(solution)/shard_map/transpose | solution.py:43
  348.5 7.4 broadcast_select_fusion.1
  355.9 8.4 %copy.150 = f32[5,9,8,34,32]{3,2,4,1,0:T(8,128)} copy(f32[5,9,8,34,32]{4,2,3,1,0:T(8,128)} %broadcast_select_fusion.1) | data formatting | bytes 3133440 | tf_op jit(solution)/shard_map/conv_general_dilated | solution.py:48
  364.3 4.2 reshape.258
  370.1 1.5 collective-permute-start.6
  371.7 14.7 %fusion.35 = f32[3,3,3,32,64]{4,3,2,1,0:T(8,128)} fusion(bf16[32,1,5,9,256]{0,1,4,3,2:T(2,128)(2,1)} %copy.153, bf16[64,1,2,4,128]{0,3,4,2,1:T(4,128)(2,1)S(1)} %fusion.97), kind=kOutput, calls=%fused_computation.49 | convolution fusion | flops 112951296 | bytes 1089536 | tf_op jit(solution)/shard_map/transpose | solution.py:43
  386.3 2.1 slice.178
  390.3 2.2 collective-permute-start.7
  392.5 88.5 %all-reduce.5.cloned.1.call-done = f32[3,3,3,64,16]{3,4,2,1,0:T(8,128)} async-done(((f32[3,3,3,64,16]{3,4,2,1,0:T(8,128)}), f32[3,3,3,64,16]{3,4,2,1,0:T(8,128)}) %all-reduce.5.cloned.1.call-update) | async-done | bytes 110608 | tf_op jit(solution)/shard_map/psum | solution.py:101
  481.0 1.6 broadcast_multiply_fusion.5
  483.7 146.6 %all-reduce.3.cloned.1.call-done = f32[3,3,3,32,64]{4,3,2,1,0:T(8,128)} async-done(((f32[3,3,3,32,64]{4,3,2,1,0:T(8,128)}), f32[3,3,3,32,64]{4,3,2,1,0:T(8,128)}) %all-reduce.3.cloned.1.call-update) | async-done | bytes 221200 | tf_op jit(solution)/shard_map/psum | solution.py:110
  630.3 1.8 broadcast_multiply_fusion.4
  632.8 1.6 fusion.34
  634.4 7.2 copy.152
  641.7 87.7 %fusion.85 = f32[3,3,3,4,32]{4,3,2,1,0:T(4,128)S(1)} fusion(bf16[4,1,9,17,512]{0,1,4,3,2:T(2,128)(2,1)} %copy.151, bf16[32,1,4,8,256]{0,1,4,3,2:T(2,128)(2,1)} %copy.152), kind=kOutput, calls=%fused_computation.116 | convolution fusion | flops 56549376 | bytes 1164800 | tf_op jit(solution)/shard_map/transpose | solution.py:43
  729.4 63.8 %psum.21 = f32[3,3,3,4,32]{4,3,2,1,0:T(4,128)S(1)} all-reduce(f32[3,3,3,4,32]{4,3,2,1,0:T(4,128)S(1)} %fusion.85), channel_id=1, replica_groups=mesh['dev'=16,'ha'=8] {'dev','ha'}, use_global_device_ids=true, to_apply=%region_1.2 | all-reduce | flops 3456 | bytes 27648 | tf_op jit(solution)/shard_map/psum | solution.py:110
  (104 shorter events, 29.8 us)
Async XLA Ops:
  7.2 130.5 %copy-start = (bf16[3,3,3,32,64]{4,3,2,1,0:T(8,128)(2,1)S(1)}, bf16[3,3,3,32,64]{4,3,2,1,0:T(8,128)(2,1)}, u32[]{:S(2)}) copy-start(bf16[3,3,3,32,64]{4,3,2,1,0:T(8,128)(2,1)} %param.13) | copy-start | bytes 331780
  7.2 192.3 %all-gather.2.cloned.1.call-start = ((), (), s32[]{:S(2)}) async-start(), calls=%async_computation.1 | async-start | bytes 1769472 | tf_op jit(solution)/shard_map/all_gather | solution.py:97
  8.1 5.9 collective-permute-start
  15.2 4.5 collective-permute-start.1
  22.9 12.0 %copy-start.15 = (bf16[3,3,3,4,32]{4,3,2,1,0:T(4,128)(2,1)S(1)}, bf16[3,3,3,4,32]{4,3,2,1,0:T(4,128)(2,1)}, u32[]{:S(2)}) copy-start(bf16[3,3,3,4,32]{4,3,2,1,0:T(4,128)(2,1)} %param.12) | copy-start | bytes 20740
  67.7 18.2 %copy-start.14 = (pred[8,33]{1,0:T(8,128)(4,1)S(1)}, pred[8,33]{1,0:T(8,128)(4,1)}, u32[]{:S(2)}) copy-start(pred[8,33]{1,0:T(8,128)(4,1)} %constant.142) | copy-start | bytes 796
  100.4 12.1 %copy-start.2 = (f32[4,8,1,264,32]{3,4,1,0,2:T(8,128)}, f32[4,8,1,264,32]{3,4,1,0,2:T(8,128)S(1)}, u32[]{:S(2)}) copy-start(f32[4,8,1,264,32]{3,4,1,0,2:T(8,128)S(1)} %reshape.226) | copy-start | bytes 3244036
  113.2 7.1 collective-permute-start.2
  120.2 5.5 collective-permute-start.3
  132.1 5.5 copy-start.16
  141.6 0.8 copy-start.4
  143.1 7.1 collective-permute-start.4
  151.5 169.6 %reduce-scatter.2.cloned.1.call-start = ((), (), s32[]{:S(2)}) async-start(), calls=%async_computation.2 | async-start | bytes 3538944 | tf_op jit(solution)/shard_map/reduce_scatter | solution.py:103
  205.9 2.4 copy-start.10
  205.9 2.4 copy-start.17
  210.6 0.9 copy-start.11
  210.6 2.2 copy-start.13
  239.1 6.3 copy-start.8
  245.3 235.7 %all-reduce.5.cloned.1.call-start = ((), (), s32[]{:S(2)}) async-start(), calls=%async_computation.4 | async-start | bytes 442368 | tf_op jit(solution)/shard_map/psum | solution.py:101
  245.3 56.0 %copy-start.9 = (bf16[32,1,5,9,256]{4,0,3,2,1:T(8,128)(2,1)S(1)}, bf16[32,1,5,9,256]{4,0,3,2,1:T(8,128)(2,1)}, u32[]{:S(2)}) copy-start(bf16[32,1,5,9,256]{4,0,3,2,1:T(8,128)(2,1)} %get-tuple-element.54) | copy-start | bytes 2211844
  301.3 9.2 %copy-start.7 = (bf16[64,3,32,128]{3,0,1,2:T(8,128)(2,1)S(1)}, bf16[64,3,32,128]{3,0,1,2:T(8,128)(2,1)}, u32[]{:S(2)}) copy-start(bf16[64,3,32,128]{3,0,1,2:T(8,128)(2,1)} %all-gather.2.cloned.1.call-done) | copy-start | bytes 4718596
  322.2 24.9 %slice-start = ((f32[64,3,4,128]{3,0,1,2:T(8,128)}), f32[64,2,4,128]{3,0,1,2:T(8,128)S(1)}, s32[]{:S(2)}) async-start(f32[64,3,4,128]{3,0,1,2:T(8,128)} %reduce-scatter.2.cloned.1.call-done), calls=%async_computation.5 | async-start | bytes 524288 | tf_op jit(solution)/shard_map/slice | solution.py:72
  322.3 25.3 %copy-start.5 = (f32[2,4,8,17,64]{4,1,3,2,0:T(4,128)S(1)}, f32[2,4,8,17,64]{4,1,3,2,0:T(4,128)}, u32[]{:S(2)}) copy-start(f32[2,4,8,17,64]{4,1,3,2,0:T(4,128)} %copy-done.4) | copy-start | bytes 835588
  322.3 25.2 %collective-permute-start.5 = (f32[64,1,4,128]{0,2,3,1:T(4,128)S(1)}, f32[64,1,4,128]{0,2,3,1:T(4,128)S(1)}, u32[]{:S(2)}, u32[]{:S(2)}) collective-permute-start(f32[64,1,4,128]{0,2,3,1:T(4,128)S(1)} %copy.168), channel_id=1, source_target_pairs={{8,0},{16,8},{24,16},{32,24},{40,32},{48,40},{56,48},{64,56},{72,6... | collective-permute-start | bytes 393224 | tf_op jit(solution)/shard_map/ppermute | solution.py:11
  346.7 1.7 copy-start.12
  346.8 283.5 %all-reduce.3.cloned.1.call-start = ((), (), s32[]{:S(2)}) async-start(), calls=%async_computation.3 | async-start | bytes 884736 | tf_op jit(solution)/shard_map/psum | solution.py:110
  368.6 1.4 copy-start.6
  370.1 18.3 %collective-permute-start.6 = (bf16[32,5,1,256]{3,0,2,1:T(8,128)(2,1)S(1)}, bf16[32,5,1,256]{3,0,2,1:T(8,128)(2,1)S(1)}, u32[]{:S(2)}, u32[]{:S(2)}) collective-permute-start(bf16[32,5,1,256]{3,0,2,1:T(8,128)(2,1)S(1)} %slice.211), channel_id=1, source_target_pairs={{1,0},{2,1},{3,2},{4,3},{5,4},{6,5},{7,6},{9,8},{10,9},{11,10},{12... | collective-permute-start | bytes 245768 | tf_op jit(solution)/shard_map/ppermute | solution.py:11
  386.3 246.5 %copy-start.3 = (f32[4,8,1,264,32]{3,4,1,0,2:T(8,128)S(1)}, f32[4,8,1,264,32]{3,4,1,0,2:T(8,128)}, u32[]{:S(2)}) copy-start(f32[4,8,1,264,32]{3,4,1,0,2:T(8,128)} %copy-done.2) | copy-start | bytes 3244036
  390.3 241.9 %collective-permute-start.7 = (f32[32,1,8,256]{3,0,2,1:T(8,128)}, f32[32,1,8,256]{3,0,2,1:T(8,128)S(1)}, u32[]{:S(2)}, u32[]{:S(2)}) collective-permute-start(f32[32,1,8,256]{3,0,2,1:T(8,128)} %slice.183), channel_id=1, source_target_pairs={{8,0},{16,8},{24,16},{32,24},{40,32},{48,40},{56,48},{64,56},{72,6... | collective-permute-start | bytes 786440 | tf_op jit(solution)/shard_map/ppermute | solution.py:11
  641.7 152.2 %copy-start.1 = (bf16[3,3,3,32,64]{4,3,2,1,0:T(8,128)(2,1)S(1)}, bf16[3,3,3,32,64]{4,3,2,1,0:T(8,128)(2,1)}, u32[]{:S(2)}) copy-start(bf16[3,3,3,32,64]{4,3,2,1,0:T(8,128)(2,1)} %param.13) | copy-start | bytes 331780
Sparse Core Ops, SparseCore 0:
  151.6 47.8 all-gather.1
  245.4 47.8 reduce-scatter.1
  346.9 134.0 all-reduce.4
  486.2 144.0 all-reduce.2
where the time goes:
time: 810 us; the launch traced here: 801 us
  waiting for transfers between devices  291 us (36%)
  local copies, waits for them, and re-layouts  210 us (26%)
  matrix products  168 us (21%)
  blocking collectives  63.8 us (8%)
  starting transfers between devices  34.9 us (4%)
  other arithmetic  18 us (2%)
  between operations  14.9 us (2%)
    psum x1, waiting for transfers between devices, local(): lax.psum((local_first, local_second), ('dev', 'ha'))  147 us
    transpose x3, matrix products, weight_grad(): return jnp.transpose(result, (2, 3, 4, 0, 1))  118 us
    psum x1, waiting for transfers between devices, local(): lax.psum(weight_grad(all_rows, delta_third, (0, 0), (1, 0)), 'dev')  88.5 us
    broadcast_in_dim x3, local copies, waits for them, and re-layouts, weight_grad(): inputs[:, None]  75.3 us
    psum x1, blocking collectives, local(): lax.psum((local_first, local_second), ('dev', 'ha'))  63.8 us
    all_gather x1, waiting for transfers between devices, local(): all_rows = lax.all_gather(deeper, 'ha', axis=2, tiled=True)  48 us
    conv_general_dilated x9, local copies, waits for them, and re-layouts, convolve(): lax.conv_general_dilated(inputs[None], kernel, (2, 2, 2), [pad_depth, pad...  43.6 us
    conv_general_dilated x3, matrix products, convolve(): lax.conv_general_dilated(inputs[None], kernel, (2, 2, 2), [pad_depth, pad...  38.7 us
  transfers between devices with their start and end apart: 12, of which 8 were waited for; matrix products, arithmetic and copies ran while one was open for 17% of the time, Pallas kernels for 0%

commit v1 on v0

--- a/solution.py
+++ b/solution.py
@@ -107,7 +107,7 @@
     back_first = retract(input_grad(delta_second, w_second)[..., 1:])
     delta_first = (back_first * leaky_slope(pre_first)).astype(jnp.bfloat16)
     local_first = weight_grad(whole_first, delta_first, (0, 0), (0, 0))
-    grad_first, grad_second = lax.psum((local_first, local_second), ("dev", "ha"))
+    grad_first, grad_second = lax.psum(lax.psum((local_first, local_second), "ha"), "dev")
     return (out_third, grad_first * scale_first, grad_second * scale_second, grad_third)
 
 

time: 810 us -> 710 us (0.88)
  waiting for transfers between devices: 291 us -> 152 us
  blocking collectives: 63.8 us -> 98.2 us
    psum x2, waiting for transfers between devices: 235 us -> 48.3 us  [the longest x1 48.3 us: local(): lax.psum((local_first, local_second), 'ha')]
    reduce_scatter x1, waiting for transfers between devices: 0.01 us -> 47.9 us  [local(): lax.psum_scatter(partial_back, 'ha', scatter_dimension=2, tiled=True)]
    psum x1 -> x2, blocking collectives: 63.8 us -> 98.2 us  [the longest x1 70.2 us: local(): lax.psum(lax.psum((local_first, local_second), 'ha'), 'dev')]
  transfers between devices with their start and end apart: 12 -> 12, of which waited for: 8 -> 8; matrix products, arithmetic and copies ran while one was open for 17% -> 30% of each run, Pallas kernels for 0% -> 0%
where the time goes in v1:
time: 710 us; the launch traced here: 696 us
  local copies, waits for them, and re-layouts  212 us (30%)
  matrix products  168 us (24%)
  waiting for transfers between devices  152 us (21%)
  blocking collectives  98.2 us (14%)
  starting transfers between devices  32.8 us (5%)
  other arithmetic  17.6 us (2%)
  between operations  14.8 us (2%)
    transpose x3, matrix products, weight_grad(): return jnp.transpose(result, (2, 3, 4, 0, 1))  118 us
    broadcast_in_dim x3, local copies, waits for them, and re-layouts, weight_grad(): inputs[:, None]  76.3 us
    psum x1, blocking collectives, local(): lax.psum(lax.psum((local_first, local_second), 'ha'), 'dev')  70.2 us
    psum x1, waiting for transfers between devices, local(): lax.psum((local_first, local_second), 'ha')  48.3 us
    all_gather x1, waiting for transfers between devices, local(): all_rows = lax.all_gather(deeper, 'ha', axis=2, tiled=True)  48 us
    reduce_scatter x1, waiting for transfers between devices, local(): lax.psum_scatter(partial_back, 'ha', scatter_dimension=2, tiled=True)  47.9 us
    conv_general_dilated x9, local copies, waits for them, and re-layouts, convolve(): lax.conv_general_dilated(inputs[None], kernel, (2, 2, 2), [pad_depth, pad...  43.5 us
    conv_general_dilated x3, matrix products, convolve(): lax.conv_general_dilated(inputs[None], kernel, (2, 2, 2), [pad_depth, pad...  38.7 us
  transfers between devices with their start and end apart: 12, of which 8 were waited for; matrix products, arithmetic and copies ran while one was open for 30% of the time, Pallas kernels for 0%

profile of v1, /device:TPU:1, one launch (start us, length us, event | category | flops | bytes accessed | tf_op | source)
XLA Modules:
  0.0 695.9 jit_solution(10084697698918230629)
XLA Ops:
  8.1 4.6 collective-permute-start
  15.2 3.1 collective-permute-start.1
  22.9 10.8 %copy.123 = bf16[4,9,17,1,8,66]{4,0,5,2,1,3:T(4,128)(2,1)} copy(bf16[4,9,17,1,8,66]{5,4,2,1,0,3:T(8,128)(2,1)S(1)} %reshape.287) | data formatting | bytes 1292544 | tf_op jit(solution)/shard_map/conv_general_dilated | solution.py:23
  35.0 32.7 %fusion.3 = f32[4,8,8,33,32]{4,2,3,1,0:T(8,128)} fusion(bf16[3,3,3,4,32]{4,3,2,1,0:T(4,128)(2,1)S(1)} %copy-done.17, bf16[4,9,17,1,7,2]{4,0,5,2,1,3:T(4,128)(2,1)S(1)} %slice.159, bf16[4,9,17,1,8,66]{4,0,5,2,1,3:T(4,128)(2,1)} %copy.123), kind=kOutput, calls=%fused_computation.4 | convolution fusion | flops 60390144 | bytes 1751664 | tf_op jit(solution)/shard_map/conv_general_dilated | solution.py:23
  67.7 18.2 %copy.124 = f32[4,8,8,33,32]{3,4,2,1,0:T(8,128)} copy(f32[4,8,8,33,32]{4,2,3,1,0:T(8,128)} %fusion.3) | data formatting | bytes 2162688 | tf_op jit(solution)/shard_map/conv_general_dilated | solution.py:23
  85.9 5.0 select_multiply_fusion
  90.9 5.8 copy.126
  96.7 3.5 reshape.226
  100.2 8.6 %copy.125 = f32[4,8,8,33,32]{3,2,4,1,0:T(8,128)} copy(f32[4,8,8,33,32]{3,4,2,1,0:T(8,128)} %get-tuple-element.55) | data formatting | bytes 2162688 | tf_op jit(solution)/shard_map/mul | solution.py:15
  108.8 3.5 reshape.224
  112.9 5.1 collective-permute-start.2
  118.1 1.9 collective-permute-done.2
  120.0 4.0 collective-permute-start.3
  127.9 4.0 reshape.229
  131.9 4.5 copy.128
  137.4 3.7 broadcast_multiply_fusion.2
  142.8 5.2 collective-permute-start.4
  148.0 1.9 collective-permute-done.4
  151.2 48.0 %all-gather.2.cloned.1.call-done = bf16[64,3,32,128]{3,0,1,2:T(8,128)(2,1)} async-done(((bf16[64,3,4,128]{3,0,1,2:T(8,128)(2,1)}), bf16[64,3,32,128]{3,0,1,2:T(8,128)(2,1)}) %all-gather.2.cloned.1.call-update) | async-done | bytes 1572880 | tf_op jit(solution)/shard_map/all_gather | solution.py:97
  199.2 5.8 copy.132
  205.7 2.3 copy.134
  208.1 2.2 broadcast_multiply_fusion
  212.6 4.3 broadcast_select_fusion
  216.8 5.9 copy.143
  222.7 8.9 %reshape.251 = f32[3,33,1,144,64]{4,3,1,0,2:T(8,128)} reshape(f32[3,33,8,18,64]{4,3,2,1,0:T(8,128)} %copy.143) | data formatting | bytes 7299072 | tf_op jit(solution)/shard_map/conv_general_dilated | solution.py:48
  231.7 3.4 slice_bitcast_fusion
  235.1 3.7 slice.172
  238.8 6.2 copy.144
  245.0 47.9 %reduce-scatter.2.cloned.1.call-done = f32[64,3,4,128]{3,0,1,2:T(8,128)} async-done(((f32[64,3,32,128]{3,0,1,2:T(8,128)}), f32[64,3,4,128]{3,0,1,2:T(8,128)}) %reduce-scatter.2.cloned.1.call-update) | async-done | bytes 393232 | tf_op jit(solution)/shard_map/reduce_scatter | solution.py:103
  294.7 6.7 collective-permute-start.5
  301.5 56.9 %copy.151 = bf16[4,1,9,17,512]{0,1,4,3,2:T(2,128)(2,1)} copy(bf16[4,1,9,17,512]{4,3,2,0,1:T(8,128)(2,1)S(1)} %copy-done.10) | data formatting | bytes 1253376 | tf_op jit(solution)/shard_map/broadcast_in_dim | solution.py:35
  358.4 8.8 %copy.153 = bf16[32,1,5,9,256]{0,1,4,3,2:T(2,128)(2,1)} copy(bf16[32,1,5,9,256]{4,0,3,2,1:T(8,128)(2,1)S(1)} %copy-done.11) | data formatting | bytes 1474560 | tf_op jit(solution)/shard_map/broadcast_in_dim | solution.py:35
  368.4 10.6 %copy.156 = bf16[64,1,3,32,128]{0,1,4,3,2:T(2,128)(2,1)} copy(bf16[64,1,3,32,128]{4,0,2,3,1:T(8,128)(2,1)S(1)} %bitcast.160) | data formatting | bytes 3145728 | tf_op jit(solution)/shard_map/broadcast_in_dim | solution.py:35
  380.4 7.3 %broadcast_select_fusion.1 = f32[5,9,8,34,32]{4,2,3,1,0:T(8,128)} fusion(pred[8,34]{0,1:T(8,128)(4,1)S(1)} %copy-done.14, bf16[3,3,3,32,64]{4,3,2,1,0:T(8,128)(2,1)S(1)} %copy-done, bf16[64,2,4,1,7,1]{0,4,5,2,1,3:T(8,128)(2,1)S(1)} %slice.176, bf16[64,2,4,1,8,17]{0,4,5,2,1,3:T(8,128)(2,1)S(1)} %copy.149), kind=kOutput, calls=%fused_computation.21 | convolution fusion | flops 121158144 | bytes 1824016 | tf_op jit(solution)/shard_map/conv_general_dilated | solution.py:48
  387.8 8.3 %copy.150 = f32[5,9,8,34,32]{3,2,4,1,0:T(8,128)} copy(f32[5,9,8,34,32]{4,2,3,1,0:T(8,128)} %broadcast_select_fusion.1) | data formatting | bytes 3133440 | tf_op jit(solution)/shard_map/conv_general_dilated | solution.py:48
  396.1 4.2 reshape.258
  401.9 1.6 collective-permute-start.6
  403.5 14.6 %fusion.35 = f32[3,3,3,32,64]{4,3,2,1,0:T(8,128)} fusion(bf16[32,1,5,9,256]{0,1,4,3,2:T(2,128)(2,1)} %copy.153, bf16[64,1,2,4,128]{0,3,4,2,1:T(4,128)(2,1)S(1)} %fusion.97), kind=kOutput, calls=%fused_computation.49 | convolution fusion | flops 112951296 | bytes 1089536 | tf_op jit(solution)/shard_map/transpose | solution.py:43
  420.6 1.7 slice.183
  422.3 2.3 collective-permute-start.7
  424.6 15.3 %fusion.86 = f32[3,3,3,64,16]{3,4,2,1,0:T(8,128)} fusion(bf16[64,1,3,32,128]{0,1,4,3,2:T(2,128)(2,1)} %copy.156, bf16[16,1,1,16,64]{0,1,4,3,2:T(2,128)(2,1)} %copy.157), kind=kOutput, calls=%fused_computation.117 | convolution fusion | flops 55154688 | bytes 1716224 | tf_op jit(solution)/shard_map/transpose | solution.py:43
  440.9 48.3 %all-reduce.4.cloned.1.call-done = f32[3,3,3,32,64]{4,3,2,1,0:T(8,128)} async-done(((f32[3,3,3,32,64]{4,3,2,1,0:T(8,128)}), f32[3,3,3,32,64]{4,3,2,1,0:T(8,128)}) %all-reduce.4.cloned.1.call-update) | async-done | bytes 221200 | tf_op jit(solution)/shard_map/psum | solution.py:110
  491.6 7.3 %copy.152 = bf16[32,1,4,8,256]{0,1,4,3,2:T(2,128)(2,1)} copy(bf16[32,1,4,8,256]{4,0,3,2,1:T(8,128)(2,1)S(1)} %fusion.34) | data formatting | bytes 1048576 | tf_op jit(solution)/shard_map/broadcast_in_dim | solution.py:36
  498.9 87.7 %fusion.85 = f32[3,3,3,4,32]{4,3,2,1,0:T(4,128)S(1)} fusion(bf16[4,1,9,17,512]{0,1,4,3,2:T(2,128)(2,1)} %copy.151, bf16[32,1,4,8,256]{0,1,4,3,2:T(2,128)(2,1)} %copy.152), kind=kOutput, calls=%fused_computation.116 | convolution fusion | flops 56549376 | bytes 1164800 | tf_op jit(solution)/shard_map/transpose | solution.py:43
  586.6 28.0 %psum.35 = f32[3,3,3,4,32]{4,3,2,1,0:T(4,128)S(1)} all-reduce(f32[3,3,3,4,32]{4,3,2,1,0:T(4,128)S(1)} %fusion.85), channel_id=1, replica_groups=mesh['dev'=16,'ha'=8] {'ha'}, use_global_device_ids=true, to_apply=%region_1.2 | all-reduce | flops 3456 | bytes 27648 | tf_op jit(solution)/shard_map/psum | solution.py:110
  614.6 70.2 %psum.36 = f32[3,3,3,4,32]{4,3,2,1,0:T(4,128)S(1)} all-reduce(f32[3,3,3,4,32]{4,3,2,1,0:T(4,128)S(1)} %psum.35), channel_id=1, replica_groups=mesh['dev'=16,'ha'=8] {'dev'}, use_global_device_ids=true, to_apply=%region_2.3 | all-reduce | flops 3456 | bytes 27648 | tf_op jit(solution)/shard_map/psum | solution.py:110
  685.4 1.8 broadcast_multiply_fusion.4
  687.2 1.6 broadcast_multiply_fusion.5
  (109 shorter events, 33.0 us)
Async XLA Ops:
  7.2 130.2 %copy-start = (bf16[3,3,3,32,64]{4,3,2,1,0:T(8,128)(2,1)S(1)}, bf16[3,3,3,32,64]{4,3,2,1,0:T(8,128)(2,1)}, u32[]{:S(2)}) copy-start(bf16[3,3,3,32,64]{4,3,2,1,0:T(8,128)(2,1)} %param.13) | copy-start | bytes 331780
  7.2 192.0 %all-gather.2.cloned.1.call-start = ((), (), s32[]{:S(2)}) async-start(), calls=%async_computation.1 | async-start | bytes 1769472 | tf_op jit(solution)/shard_map/all_gather | solution.py:97
  8.1 5.9 collective-permute-start
  15.2 4.5 collective-permute-start.1
  22.9 12.0 %copy-start.17 = (bf16[3,3,3,4,32]{4,3,2,1,0:T(4,128)(2,1)S(1)}, bf16[3,3,3,4,32]{4,3,2,1,0:T(4,128)(2,1)}, u32[]{:S(2)}) copy-start(bf16[3,3,3,4,32]{4,3,2,1,0:T(4,128)(2,1)} %param.12) | copy-start | bytes 20740
  67.7 18.2 %copy-start.16 = (pred[8,33]{1,0:T(8,128)(4,1)S(1)}, pred[8,33]{1,0:T(8,128)(4,1)}, u32[]{:S(2)}) copy-start(pred[8,33]{1,0:T(8,128)(4,1)} %constant.142) | copy-start | bytes 796
  100.2 12.1 %copy-start.2 = (f32[4,8,1,264,32]{3,4,1,0,2:T(8,128)}, f32[4,8,1,264,32]{3,4,1,0,2:T(8,128)S(1)}, u32[]{:S(2)}) copy-start(f32[4,8,1,264,32]{3,4,1,0,2:T(8,128)S(1)} %reshape.226) | copy-start | bytes 3244036
  112.9 7.1 %collective-permute-start.2 = (bf16[32,1,8,256]{3,0,2,1:T(8,128)(2,1)S(1)}, bf16[32,1,8,256]{3,0,2,1:T(8,128)(2,1)S(1)}, u32[]{:S(2)}, u32[]{:S(2)}) collective-permute-start(bf16[32,1,8,256]{3,0,2,1:T(8,128)(2,1)S(1)} %slice.162), channel_id=1, source_target_pairs={{0,8},{8,16},{16,24},{24,32},{32,40},{40,48},{48,56},{56,64},{64,7... | collective-permute-start | bytes 393224 | tf_op jit(solution)/shard_map/ppermute | solution.py:11
  120.0 5.5 collective-permute-start.3
  131.9 5.5 copy-start.18
  141.3 0.8 copy-start.4
  142.8 7.1 %collective-permute-start.4 = (bf16[64,1,4,128]{0,2,3,1:T(4,128)(2,1)S(1)}, bf16[64,1,4,128]{0,2,3,1:T(4,128)(2,1)S(1)}, u32[]{:S(2)}, u32[]{:S(2)}) collective-permute-start(bf16[64,1,4,128]{0,2,3,1:T(4,128)(2,1)S(1)} %slice.166), channel_id=1, source_target_pairs={{0,8},{8,16},{16,24},{24,32},{32,40},{40,48},{48,56},{56,64},{64,7... | collective-permute-start | bytes 196616 | tf_op jit(solution)/shard_map/ppermute | solution.py:11
  151.2 141.7 %reduce-scatter.2.cloned.1.call-start = ((), (), s32[]{:S(2)}) async-start(), calls=%async_computation.2 | async-start | bytes 3538944 | tf_op jit(solution)/shard_map/reduce_scatter | solution.py:103
  205.6 2.4 copy-start.12
  205.6 2.4 copy-start.19
  210.3 0.9 copy-start.13
  210.3 2.2 copy-start.15
  245.0 56.5 %copy-start.10 = (bf16[4,1,9,17,512]{4,3,2,0,1:T(8,128)(2,1)S(1)}, bf16[4,1,9,17,512]{4,3,2,0,1:T(8,128)(2,1)}, u32[]{:S(2)}) copy-start(bf16[4,1,9,17,512]{4,3,2,0,1:T(8,128)(2,1)} %get-tuple-element.58) | copy-start | bytes 1880068
  245.0 244.3 %all-reduce.4.cloned.1.call-start = ((), (), s32[]{:S(2)}) async-start(), calls=%async_computation.3 | async-start | bytes 884736 | tf_op jit(solution)/shard_map/psum | solution.py:110
  294.7 84.6 %collective-permute-start.5 = (f32[64,1,4,128]{0,2,3,1:T(4,128)}, f32[64,1,4,128]{0,2,3,1:T(4,128)S(1)}, u32[]{:S(2)}, u32[]{:S(2)}) collective-permute-start(f32[64,1,4,128]{0,2,3,1:T(4,128)} %copy.168), channel_id=1, source_target_pairs={{8,0},{16,8},{24,16},{32,24},{40,32},{48,40},{56,48},{64,56},{72,6... | collective-permute-start | bytes 393224 | tf_op jit(solution)/shard_map/ppermute | solution.py:11
  301.5 56.9 %copy-start.11 = (bf16[32,1,5,9,256]{4,0,3,2,1:T(8,128)(2,1)S(1)}, bf16[32,1,5,9,256]{4,0,3,2,1:T(8,128)(2,1)}, u32[]{:S(2)}) copy-start(bf16[32,1,5,9,256]{4,0,3,2,1:T(8,128)(2,1)} %get-tuple-element.56) | copy-start | bytes 2211844
  358.4 10.0 %copy-start.9 = (bf16[64,3,32,128]{3,0,1,2:T(8,128)(2,1)S(1)}, bf16[64,3,32,128]{3,0,1,2:T(8,128)(2,1)}, u32[]{:S(2)}) copy-start(bf16[64,3,32,128]{3,0,1,2:T(8,128)(2,1)} %all-gather.2.cloned.1.call-done) | copy-start | bytes 4718596
  368.4 10.8 %slice-start = ((f32[64,3,4,128]{3,0,1,2:T(8,128)}), f32[64,2,4,128]{3,0,1,2:T(8,128)S(1)}, s32[]{:S(2)}) async-start(f32[64,3,4,128]{3,0,1,2:T(8,128)} %reduce-scatter.2.cloned.1.call-done), calls=%async_computation.5 | async-start | bytes 524288 | tf_op jit(solution)/shard_map/slice | solution.py:72
  368.4 11.1 %copy-start.5 = (f32[2,4,8,17,64]{4,1,3,2,0:T(4,128)S(1)}, f32[2,4,8,17,64]{4,1,3,2,0:T(4,128)}, u32[]{:S(2)}) copy-start(f32[2,4,8,17,64]{4,1,3,2,0:T(4,128)} %copy-done.4) | copy-start | bytes 835588
  379.0 1.5 copy-start.14
  400.4 1.4 copy-start.6
  401.9 16.3 %copy-start.7 = (f32[32,5,9,257]{3,0,2,1:T(8,128)S(1)}, f32[32,5,9,257]{3,0,2,1:T(8,128)}, u32[]{:S(2)}) copy-start(f32[32,5,9,257]{3,0,2,1:T(8,128)} %copy-done.6) | copy-start | bytes 4440964
  401.9 17.9 %collective-permute-start.6 = (bf16[32,5,1,256]{3,0,2,1:T(8,128)(2,1)S(1)}, bf16[32,5,1,256]{3,0,2,1:T(8,128)(2,1)S(1)}, u32[]{:S(2)}, u32[]{:S(2)}) collective-permute-start(bf16[32,5,1,256]{3,0,2,1:T(8,128)(2,1)S(1)} %slice.211), channel_id=1, source_target_pairs={{1,0},{2,1},{3,2},{4,3},{5,4},{6,5},{7,6},{9,8},{10,9},{11,10},{12... | collective-permute-start | bytes 245768 | tf_op jit(solution)/shard_map/ppermute | solution.py:11
  419.7 265.7 %all-reduce.6.cloned.1.call-start = ((), (), s32[]{:S(2)}) async-start(), calls=%async_computation.4 | async-start | bytes 1327104 | tf_op jit(solution)/shard_map/psum | solution.py:110
  422.3 17.6 %copy-start.8 = (f32[32,5,8,256]{3,0,2,1:T(8,128)S(1)}, f32[32,5,8,256]{3,0,2,1:T(8,128)}, u32[]{:S(2)}) copy-start(f32[32,5,8,256]{3,0,2,1:T(8,128)} %fusion.52) | copy-start | bytes 3932164
  422.3 67.0 %collective-permute-start.7 = (f32[32,1,8,256]{3,0,2,1:T(8,128)}, f32[32,1,8,256]{3,0,2,1:T(8,128)S(1)}, u32[]{:S(2)}, u32[]{:S(2)}) collective-permute-start(f32[32,1,8,256]{3,0,2,1:T(8,128)} %slice.183), channel_id=1, source_target_pairs={{8,0},{16,8},{24,16},{32,24},{40,32},{48,40},{56,48},{64,56},{72,6... | collective-permute-start | bytes 786440 | tf_op jit(solution)/shard_map/ppermute | solution.py:11
  439.9 50.2 %copy-start.3 = (f32[4,8,1,264,32]{3,4,1,0,2:T(8,128)S(1)}, f32[4,8,1,264,32]{3,4,1,0,2:T(8,128)}, u32[]{:S(2)}) copy-start(f32[4,8,1,264,32]{3,4,1,0,2:T(8,128)} %copy-done.2) | copy-start | bytes 3244036
  498.9 190.0 %copy-start.1 = (bf16[3,3,3,32,64]{4,3,2,1,0:T(8,128)(2,1)S(1)}, bf16[3,3,3,32,64]{4,3,2,1,0:T(8,128)(2,1)}, u32[]{:S(2)}) copy-start(bf16[3,3,3,32,64]{4,3,2,1,0:T(8,128)(2,1)} %param.13) | copy-start | bytes 331780
Sparse Core Ops, SparseCore 0:
  151.3 47.8 all-gather.1
  245.1 47.7 reduce-scatter.1
  419.8 69.3 all-reduce.3
  492.2 142.0 all-reduce.5
